TPU v7x, 32 devices: a whole 2x2x4 slice. The times are simulated.
32 devices in a mesh: groups: 2 (over y), row: 4 (over z), col: 2 (over x), mp: 2 (over core).
Axes of the slice: x: 2, y: 2, z: 4, core: 2. Of those that a mesh axis runs over, the one named last changes fastest.
Arguments:
- queries: bfloat16 [2, 2048, 5120], P('mp', ('groups', 'row'), 'col'), parts along dimension 1, may hold values from -6 to 6
- keys: bfloat16 [2, 2048, 1024], P('mp', ('groups', 'row'), 'col'), parts along dimension 1, may hold values from -6 to 6
- values: bfloat16 [2, 2048, 1024], P('mp', ('groups', 'row'), 'col'), parts along dimension 1, may hold values from -6 to 6
- lengths: int32 [4], P('groups'), parts along dimension 0, may hold values from 1 to 768, 1024 in all
Outputs:
- outputs: bfloat16 [2, 2048, 5120], P('mp', ('groups', 'row'), 'col'), parts along dimension 1
- gap: float32 [40, 2048], P(('col', 'mp'), ('groups', 'row')), parts along dimension 1
There are 2 independent parts, one for each index of `groups`. A program takes and returns all parts, laid end to end along the dimension named above; each array names one. Nothing has to cross between parts.
Inputs may be any that keep to these rules, and one draw needn't show every extreme that they name: The 2 lengths sum to 1024; one rollout is exactly 768 tokens long.
All inputs are finite; a program needn't handle non-finite values.
Results may differ from a plain program's by a relative error of at most 0.011.
Values may be sent and summed in bfloat16 or wider, within the bound.
A program may use at most 64 MiB of HBM per device.

v0:
```python
import math

import jax
import jax.numpy as jnp
from jax import lax
from jax.sharding import PartitionSpec as P

HEADS = 40
KV_HEADS = 8
HEAD_DIM = 128


def from_behind(block, axis, distance):
    devices = range(lax.axis_size(axis))
    route = [(i - distance, i) for i in devices if i - distance in devices]
    return lax.ppermute(block, axis, route)


def swapped(block, axis, distance):
    count = lax.axis_size(axis)
    route = []
    for low in range(count):
        high = low | 1 << distance
        if high != low and high < count:
            route += [(low, high), (high, low)]
    return lax.ppermute(block, axis, route)


def relative_gap(first, second, tokens_here, heads_count):
    first = first.astype(jnp.float32).reshape(tokens_here, heads_count, HEAD_DIM)
    second = second.astype(jnp.float32).reshape(tokens_here, heads_count, HEAD_DIM)
    difference = first - second
    scale_sum = jnp.mean(first * first, axis=-1) + 1e-06
    return jnp.transpose(jnp.mean(difference * difference, axis=-1) / scale_sum)


def per_device(queries, keys, values, lengths):
    tokens_here = queries.shape[1]
    width_here = keys.shape[2]
    kv_local = width_here // HEAD_DIM
    group_size = HEADS // KV_HEADS
    heads_local = kv_local * group_size
    factor = 1.0 / math.sqrt(HEAD_DIM)
    row_pos = lax.axis_index("row")
    first_pos = row_pos * tokens_here
    query_pos = first_pos + jnp.arange(tokens_here, dtype=jnp.int32)
    finish = jnp.cumsum(lengths)
    begin_at = jnp.sum(
        jnp.where(finish[None, :] <= query_pos[:, None], lengths[None, :], 0), axis=1
    )
    lowest = begin_at[0]
    highest = first_pos + tokens_here - 1
    query_rows = queries[0].reshape(tokens_here, kv_local, group_size, HEAD_DIM)

    def update(running, stacked, offset):
        best, summed, accum = running
        amount = stacked.shape[1]
        key_rows = stacked[0].reshape(amount, kv_local, HEAD_DIM)
        value_rows = stacked[1].reshape(amount, kv_local, HEAD_DIM)
        scores = (
            jnp.einsum("tkgd,nkd->kgtn", query_rows, key_rows, preferred_element_type=jnp.float32)
            * factor
        )
        key_pos = offset + jnp.arange(amount, dtype=jnp.int32)
        allowed = (key_pos[None, :] >= begin_at[:, None]) & (key_pos[None, :] <= query_pos[:, None])
        masked = jnp.where(allowed, scores, -jnp.inf)
        fresh_best = jnp.maximum(best, jnp.max(masked, axis=-1))
        weights = jnp.where(allowed, jnp.exp(masked - fresh_best[..., None]), 0.0)
        shrink = jnp.exp(best - fresh_best)
        summed = summed * shrink + jnp.sum(weights, axis=-1)
        accum = accum * shrink[..., None] + jnp.einsum(
            "kgtn,nkd->kgtd",
            weights.astype(jnp.bfloat16),
            value_rows,
            preferred_element_type=jnp.float32,
        )
        return (fresh_best, summed, accum)

    def absorb(running, stacked, offset):
        amount = stacked.shape[1]
        needed = (offset + amount > lowest) & (offset <= highest)
        return lax.cond(
            needed, lambda inner: update(inner, stacked, offset), lambda inner: inner, running
        )

    start_state = (
        jnp.full((kv_local, group_size, tokens_here), -1e30, jnp.float32),
        jnp.zeros((kv_local, group_size, tokens_here), jnp.float32),
        jnp.zeros((kv_local, group_size, tokens_here, HEAD_DIM), jnp.float32),
    )
    paired = jnp.concatenate([keys, values], axis=0)
    reach = lax.axis_size("row") // 2 + 1
    running = absorb(start_state, paired, first_pos)

    def advance(step_id, loop_state):
        inner, moving = loop_state
        moving = from_behind(moving, "row", 1)
        return (absorb(inner, moving, (row_pos - step_id) * tokens_here), moving)

    running, _ = lax.fori_loop(1, reach + 1, advance, (running, paired))
    best, summed, accum = running
    mixed = accum / summed[..., None]
    outputs = (
        jnp.transpose(mixed, (2, 0, 1, 3))
        .reshape(tokens_here, heads_local * HEAD_DIM)
        .astype(jnp.bfloat16)[None]
    )
    half_heads = heads_local // 2
    partner = swapped(outputs, "mp", 0)
    model_pos = lax.axis_index("mp")
    is_policy = model_pos == 0
    policy = jnp.where(is_policy, outputs[0], partner[0])
    anchor = jnp.where(is_policy, partner[0], outputs[0])
    column_at = model_pos * half_heads * HEAD_DIM
    policy_part = lax.dynamic_slice_in_dim(policy, column_at, half_heads * HEAD_DIM, 1)
    anchor_part = lax.dynamic_slice_in_dim(anchor, column_at, half_heads * HEAD_DIM, 1)
    gap = relative_gap(policy_part, anchor_part, tokens_here, half_heads)
    return (outputs, gap)


def solution(mesh):
    in_specs = (
        P("mp", ("groups", "row"), "col"),
        P("mp", ("groups", "row"), "col"),
        P("mp", ("groups", "row"), "col"),
        P("groups"),
    )
    out_specs = (P("mp", ("groups", "row"), "col"), P(("col", "mp"), ("groups", "row")))
    return jax.shard_map(
        per_device, mesh=mesh, in_specs=in_specs, out_specs=out_specs, check_vma=False
    )
```

profile of v0, /device:TPU:18, one launch (start us, length us, event | category | flops | bytes accessed | tf_op | source)
XLA Modules:
  0.0 102.0 jit_solution(17828449757495927564)
XLA Ops:
  0.6 0.0 copy-start.2
  0.6 0.0 copy-start.1
  0.7 0.9 reduce-window.8
  1.5 0.7 fusion.38
  2.3 0.6 slice.9
  2.9 1.6 %copy.31 = bf16[1,256,2560]{1,2,0:T(8,128)(2,1)S(1)} copy(bf16[1,256,2560]{2,1,0:T(8,128)(2,1)} %param.10) | data formatting | bytes 2621440 | tf_op args[0]
  4.5 1.1 %copy.34 = bf16[1,256,512]{1,2,0:T(8,128)(2,1)S(1)} copy(bf16[1,256,512]{2,1,0:T(8,128)(2,1)} %param.12) | data formatting | bytes 524288 | tf_op args[2]
  5.6 1.8 %copy.33 = bf16[1,256,512]{1,2,0:T(8,128)(2,1)} copy(bf16[1,256,512]{2,1,0:T(8,128)(2,1)} %param.11) | data formatting | bytes 524288 | tf_op args[1]
  7.3 0.8 copy.35
  8.8 1.8 %pad_maximum_fusion = bf16[2,256,512]{1,2,0:T(8,128)(2,1)} fusion(bf16[1,256,512]{1,2,0:T(8,128)(2,1)S(1)} %copy.34, bf16[1,256,512]{1,2,0:T(8,128)(2,1)} %copy.33), kind=kLoop, calls=%fused_computation.49 | loop fusion | flops 262144 | bytes 1048576 | tf_op jit(solution)/shard_map/concatenate | solution.py:91
  10.6 12.4 %conditional.2 = (f32[4,5,256]{2,1,0:T(8,128)}, f32[4,5,256]{2,1,0:T(8,128)S(1)}, f32[4,5,256,128]{3,2,1,0:T(8,128)}) conditional(s32[]{:T(128)} %convert_element_type.42, () %tuple.37, (s32[]{:T(128)}, s32[256]{0:T(256)S(1)}, s32[256]{0:T(256)S(1)}, bf16[1,256,512]{2,1,0:T(8,128)(2,1)S(1)}, bf16[256,4,5,128]{0,3,2,1:T(8,128)(2,1)S(1)}, ...), branch_computations={%region_2.3_spmd, %region_3.6_spmd} | conditional | flops 689000704 | bytes 42696760 | solution.py:82
  10.6 0.1 compare_and_fusion
  10.8 0.1 squeeze.9
  10.8 0.9 fusion.2
  11.7 0.7 exponential_multiply_fusion
  12.4 1.7 %copy-done = f32[4,256,256,5]{2,1,3,0:T(8,128)} copy-done((f32[4,256,256,5]{2,1,3,0:T(8,128)}, f32[4,256,256,5]{2,1,3,0:T(8,128)S(1)}, u32[]{:S(2)}) %copy-start) | copy-done | bytes 5242904 | tf_op jit(solution)/shard_map/cond
  14.1 2.0 %fusion.4 = f32[4,5,256]{2,1,0:T(8,128)S(1)} fusion(f32[4,256,256,5]{2,1,3,0:T(8,128)S(1)} %get-tuple-element.348, f32[4,5,256]{2,1,0:T(8,128)} %get-tuple-element.439, pred[256,256]{0,1:T(8,128)(4,1)S(1)} %compare_and_fusion), kind=kLoop, calls=%fused_computation.5 | loop fusion | flops 6548480 | bytes 5349376 | tf_op jit(solution)/shard_map/cond/branch_1_fun/reduce_sum | solution.py:70
  16.1 0.8 fusion.21
  16.8 0.1 squeeze.14
  16.9 6.1 %fusion.12 = f32[4,5,256,128]{3,2,1,0:T(8,128)} fusion(f32[4,256,256,5]{2,1,3,0:T(8,128)} %copy-done, f32[4,5,256]{2,1,0:T(8,128)} %get-tuple-element.439, pred[256,256]{0,1:T(8,128)(4,1)S(1)} %compare_and_fusion, f32[4,5,256]{2,1,0:T(8,128)S(1)} %get-tuple-element.343, bf16[256,4,128,1]{2,1,0,3:T(4,128)(2,1)S(1)} %bitcast.67), kind=kOutput, calls=%fused_computation.12 | convolution fusion | flops 342753280 | bytes 8232960 | tf_op jit(solution)/shard_map/cond/branch_1_fun/kgtn,nkd->kgtd/dot_general | solution.py:71
  23.0 64.9 %while.20 = (s32[]{:T(128)}, f32[4,5,256]{2,1,0:T(8,128)}, f32[4,5,256]{2,1,0:T(8,128)S(1)}, f32[4,5,256,128]{3,2,1,0:T(8,128)}, bf16[2,256,512]{1,2,0:T(8,128)(...) while((s32[]{:T(128)}, f32[4,5,256]{2,1,0:T(8,128)}, ...), condition=%wide.region_11.12_spmd.clone, body=%wide.region_6.11_spmd.clone.sunk | while | flops 689646080 | bytes 27598188 | solution.py:100
  23.0 3.5 %collective-permute-start = (bf16[2,256,512]{1,2,0:T(8,128)(2,1)}, bf16[2,256,512]{1,2,0:T(8,128)(2,1)S(1)}, u32[]{:S(2)}, u32[]{:S(2)}) collective-permute-start(bf16[2,256,512]{1,2,0:T(8,128)(2,1)} %get-tuple-element.459), channel_id=1, source_target_pairs={{0,4},{4,8},{8,12},{1,5},{5,9},{9,13},{2,6},{6,10},{10,14},{3,7},{... | collective-permute-start | bytes 1572872 | tf_op jit(solution)/shard_map/while/body/eval_jaxpr/ppermute | solution.py:16
  27.2 11.6 %collective-permute-done = bf16[2,256,512]{1,2,0:T(8,128)(2,1)S(1)} collective-permute-done((bf16[2,256,512]{1,2,0:T(8,128)(2,1)}, bf16[2,256,512]{1,2,0:T(8,128)(2,1)S(1)}, u32[]{:S(2)}, u32[]{:S(2)}) %collective-permute-start) | collective-permute-done | bytes 524320 | tf_op jit(solution)/shard_map/while/body/eval_jaxpr/ppermute | solution.py:16
  38.8 9.3 %conditional.5 = ((f32[4,5,256]{2,1,0:T(8,128)}, f32[4,5,256]{2,1,0:T(8,128)S(1)}, f32[4,5,256,128]{3,2,1,0:T(8,128)})) conditional(s32[]{:T(128)} %convert_element_type.65, (f32[4,5,256]{2,1,0:T(8,128)}, f32[4,5,256]{2,1,0:T(8,128)S(1)}, f32[4,5,256,128]{3,2,1,0:T(8,128)}) %tuple.69, (s32[]{:T(128)}, s32[256]{0:T(256)S(1)}, s32[]{:T(128)}, ...), branch_computations={%region_7.7_spmd, %region_8.10_spmd} | conditional | flops 689646080 | bytes 24451112 | solution.py:82
  38.8 0.1 compare_and_fusion.1
  39.0 1.0 %fusion.22 = (f32[4,5,256]{2,1,0:T(8,128)S(1)}, f32[4,256,256,5]{2,1,3,0:T(8,128)S(1)}) fusion(pred[256,256]{0,1:T(8,128)(4,1)S(1)} %compare_and_fusion.1, bf16[256,4,128,1]{0,2,3,1:T(8,128)(2,1)S(1)} %bitcast.56, bf16[256,4,5,128]{3,0,2,1:T(8,128)(2,1)S(1)} %get-tuple-element.222), kind=kOutput, calls=%fused_computation.26 | convolution fusion | flops 339471360 | bytes 6901760 | tf_op jit(solution)/shard_map/while/body/eval_jaxpr/cond/branch_1_fun/tkgd,nkd->kgtn/dot_general | solution.py:61
  40.0 0.8 max.2
  40.8 1.3 %fusion.24 = f32[4,5,256]{2,1,0:T(8,128)S(1)} fusion(f32[4,256,256,5]{2,1,3,0:T(8,128)S(1)} %get-tuple-element.352, f32[4,5,256]{2,1,0:T(8,128)S(1)} %max.2, pred[256,256]{0,1:T(8,128)(4,1)S(1)} %compare_and_fusion.1), kind=kLoop, calls=%fused_computation.28 | loop fusion | flops 6548480 | bytes 5349376 | tf_op jit(solution)/shard_map/while/body/eval_jaxpr/cond/branch_1_fun/reduce_sum | solution.py:70
  42.0 0.8 multiply_add_fusion.1
  42.8 0.6 copy.62
  43.4 4.7 %multiply_add_fusion = f32[4,5,256,128]{3,2,1,0:T(8,128)} fusion(f32[4,5,256,128]{3,2,1,0:T(8,128)} %get-tuple-element.224, bf16[256,4,128,1]{0,2,3,1:T(8,128)(2,1)S(1)} %bitcast.62, f32[4,256,256,5]{2,1,3,0:T(8,128)S(1)} %get-tuple-element.352, f32[4,5,256]{2,1,0:T(8,128)S(1)} %max.2, pred[256,256]{0,1:T(8,128)(4,1)S(1)} %compare_and_fusion.1, ...), kind=kOutput, calls=%fused_computation.30 | convolution fusion | flops 343408640 | bytes 10854400 | tf_op jit(solution)/shard_map/while/body/eval_jaxpr/cond/branch_1_fun/kgtn,nkd->kgtd/dot_general | solution.py:71
  48.1 0.8 copy.85
  48.9 3.5 %collective-permute-start = (bf16[2,256,512]{1,2,0:T(8,128)(2,1)}, bf16[2,256,512]{1,2,0:T(8,128)(2,1)S(1)}, u32[]{:S(2)}, u32[]{:S(2)}) collective-permute-start(bf16[2,256,512]{1,2,0:T(8,128)(2,1)} %get-tuple-element.459), channel_id=1, source_target_pairs={{0,4},{4,8},{8,12},{1,5},{5,9},{9,13},{2,6},{6,10},{10,14},{3,7},{... | collective-permute-start | bytes 1572872 | tf_op jit(solution)/shard_map/while/body/eval_jaxpr/ppermute | solution.py:16
  53.1 10.7 %collective-permute-done = bf16[2,256,512]{1,2,0:T(8,128)(2,1)S(1)} collective-permute-done((bf16[2,256,512]{1,2,0:T(8,128)(2,1)}, bf16[2,256,512]{1,2,0:T(8,128)(2,1)S(1)}, u32[]{:S(2)}, u32[]{:S(2)}) %collective-permute-start) | collective-permute-done | bytes 524320 | tf_op jit(solution)/shard_map/while/body/eval_jaxpr/ppermute | solution.py:16
  63.8 0.8 copy.85
  64.6 12.8 %collective-permute-start = (bf16[2,256,512]{1,2,0:T(8,128)(2,1)}, bf16[2,256,512]{1,2,0:T(8,128)(2,1)S(1)}, u32[]{:S(2)}, u32[]{:S(2)}) collective-permute-start(bf16[2,256,512]{1,2,0:T(8,128)(2,1)} %get-tuple-element.459), channel_id=1, source_target_pairs={{0,4},{4,8},{8,12},{1,5},{5,9},{9,13},{2,6},{6,10},{10,14},{3,7},{... | collective-permute-start | bytes 1572872 | tf_op jit(solution)/shard_map/while/body/eval_jaxpr/ppermute | solution.py:16
  78.1 9.1 %collective-permute-done = bf16[2,256,512]{1,2,0:T(8,128)(2,1)S(1)} collective-permute-done((bf16[2,256,512]{1,2,0:T(8,128)(2,1)}, bf16[2,256,512]{1,2,0:T(8,128)(2,1)S(1)}, u32[]{:S(2)}, u32[]{:S(2)}) %collective-permute-start) | collective-permute-done | bytes 524320 | tf_op jit(solution)/shard_map/while/body/eval_jaxpr/ppermute | solution.py:16
  87.2 0.8 copy.85
  88.0 3.2 %copy.36 = f32[4,5,256,128]{2,3,1,0:T(8,128)} copy(f32[4,5,256,128]{3,2,1,0:T(8,128)} %get-tuple-element.250) | data formatting | bytes 5242880 | tf_op jit(solution)/shard_map/while | solution.py:100
  91.2 2.0 %divide_convert_fusion = bf16[4,5,256,128]{2,3,1,0:T(8,128)(2,1)S(1)} fusion(f32[4,5,256,128]{2,3,1,0:T(8,128)} %copy.36, f32[4,5,256]{2,1,0:T(8,128)S(1)} %get-tuple-element.251), kind=kLoop, calls=%fused_computation.44 | loop fusion | flops 1310720 | bytes 3952640 | tf_op jit(solution)/shard_map/convert_element_type | solution.py:106
  93.2 0.1 collective-permute-start.1
  93.3 1.6 %copy.37 = bf16[1,256,2560]{2,1,0:T(8,128)(2,1)} copy(bf16[1,256,2560]{1,2,0:T(8,128)(2,1)S(1)} %bitcast.60) | data formatting | bytes 2621440
  94.9 1.4 %collective-permute-done.1 = bf16[1,256,2560]{1,2,0:T(8,128)(2,1)S(1)} collective-permute-done((bf16[1,256,2560]{1,2,0:T(8,128)(2,1)S(1)}, bf16[1,256,2560]{1,2,0:T(8,128)(2,1)S(1)}, u32[]{:S(2)}, u32[]{:S(2)}) %collective-permute-start.1) | collective-permute-done | bytes 1310752 | tf_op jit(solution)/shard_map/ppermute | solution.py:26
  96.3 1.1 %copy-done.3 = bf16[1,256,2560]{1,2,0:T(8,128)(2,1)} copy-done((bf16[1,256,2560]{1,2,0:T(8,128)(2,1)}, bf16[1,256,2560]{1,2,0:T(8,128)(2,1)S(1)}, u32[]{:S(2)}) %copy-start.3) | copy-done | bytes 1310744
  97.4 2.5 %fusion.37 = (f32[256,1280]{0,1:T(8,128)S(1)}, f32[256,1280]{0,1:T(8,128)}) fusion(pred[]{:T(512)S(6)} %eq.3, bf16[256,2560]{0,1:T(8,128)(2,1)} %bitcast.66, s32[]{:T(128)S(6)} %select_n.36, bf16[256,2560]{0,1:T(8,128)(2,1)S(1)} %bitcast.61), kind=kLoop, calls=%fused_computation.47 | loop fusion | flops 2293760 | bytes 3932165 | tf_op jit(solution)/shard_map/mul | solution.py:34
  99.8 1.4 %reduce_sum.47 = f32[256,10]{0,1:T(8,128)S(1)} reduce(f32[256,10,128]{0,2,1:T(8,128)} %bitcast.64, f32[]{:T(128)} %constant.68.clone.1), dimensions={2}, to_apply=%region_13.14 | reduce | flops 325120 | bytes 1320964 | tf_op jit(solution)/shard_map/reduce_sum | solution.py:33
  101.3 0.1 reduce_sum.46
  101.4 0.6 divide_bitcast_fusion
  (13 shorter events, 0.1 us)
Async XLA Ops:
  0.6 8.2 %copy-start.2 = (bf16[1,256,512]{2,1,0:T(8,128)(2,1)S(1)}, bf16[1,256,512]{2,1,0:T(8,128)(2,1)}, u32[]{:S(2)}) copy-start(bf16[1,256,512]{2,1,0:T(8,128)(2,1)} %param.12) | copy-start | bytes 786436
  0.6 8.2 %copy-start.1 = (bf16[1,256,512]{2,1,0:T(8,128)(2,1)S(1)}, bf16[1,256,512]{2,1,0:T(8,128)(2,1)}, u32[]{:S(2)}) copy-start(bf16[1,256,512]{2,1,0:T(8,128)(2,1)} %param.11) | copy-start | bytes 786436
  11.7 2.3 %copy-start = (f32[4,256,256,5]{2,1,3,0:T(8,128)}, f32[4,256,256,5]{2,1,3,0:T(8,128)S(1)}, u32[]{:S(2)}) copy-start(f32[4,256,256,5]{2,1,3,0:T(8,128)S(1)} %get-tuple-element.348) | copy-start | bytes 15728644 | tf_op jit(solution)/shard_map/cond
  23.0 15.8 %collective-permute-start = (bf16[2,256,512]{1,2,0:T(8,128)(2,1)}, bf16[2,256,512]{1,2,0:T(8,128)(2,1)S(1)}, u32[]{:S(2)}, u32[]{:S(2)}) collective-permute-start(bf16[2,256,512]{1,2,0:T(8,128)(2,1)} %get-tuple-element.459), channel_id=1, source_target_pairs={{0,4},{4,8},{8,12},{1,5},{5,9},{9,13},{2,6},{6,10},{10,14},{3,7},{... | collective-permute-start | bytes 1572872 | tf_op jit(solution)/shard_map/while/body/eval_jaxpr/ppermute | solution.py:16
  48.9 14.9 %collective-permute-start = (bf16[2,256,512]{1,2,0:T(8,128)(2,1)}, bf16[2,256,512]{1,2,0:T(8,128)(2,1)S(1)}, u32[]{:S(2)}, u32[]{:S(2)}) collective-permute-start(bf16[2,256,512]{1,2,0:T(8,128)(2,1)} %get-tuple-element.459), channel_id=1, source_target_pairs={{0,4},{4,8},{8,12},{1,5},{5,9},{9,13},{2,6},{6,10},{10,14},{3,7},{... | collective-permute-start | bytes 1572872 | tf_op jit(solution)/shard_map/while/body/eval_jaxpr/ppermute | solution.py:16
  64.6 22.6 %collective-permute-start = (bf16[2,256,512]{1,2,0:T(8,128)(2,1)}, bf16[2,256,512]{1,2,0:T(8,128)(2,1)S(1)}, u32[]{:S(2)}, u32[]{:S(2)}) collective-permute-start(bf16[2,256,512]{1,2,0:T(8,128)(2,1)} %get-tuple-element.459), channel_id=1, source_target_pairs={{0,4},{4,8},{8,12},{1,5},{5,9},{9,13},{2,6},{6,10},{10,14},{3,7},{... | collective-permute-start | bytes 1572872 | tf_op jit(solution)/shard_map/while/body/eval_jaxpr/ppermute | solution.py:16
  93.2 3.1 %collective-permute-start.1 = (bf16[1,256,2560]{1,2,0:T(8,128)(2,1)S(1)}, bf16[1,256,2560]{1,2,0:T(8,128)(2,1)S(1)}, u32[]{:S(2)}, u32[]{:S(2)}) collective-permute-start(bf16[1,256,2560]{1,2,0:T(8,128)(2,1)S(1)} %bitcast.59), channel_id=1, source_target_pairs={{0,1},{1,0},{2,3},{3,2},{4,5},{5,4},{6,7},{7,6},{8,9},{9,8},{10,11... | collective-permute-start | bytes 3932168 | tf_op jit(solution)/shard_map/ppermute | solution.py:26
  96.3 1.1 %copy-start.3 = (bf16[1,256,2560]{1,2,0:T(8,128)(2,1)}, bf16[1,256,2560]{1,2,0:T(8,128)(2,1)S(1)}, u32[]{:S(2)}) copy-start(bf16[1,256,2560]{1,2,0:T(8,128)(2,1)S(1)} %collective-permute-done.1) | copy-start | bytes 3932164
where the time goes:
time: 104 us; the launch traced here: 102 us
  waiting for transfers between devices  32.8 us (32%)
  starting transfers between devices  19.8 us (19%)
  local copies, waits for them, and re-layouts  16.5 us (16%)
  other arithmetic  16.5 us (16%)
  matrix products  12.7 us (12%)
  loops' own time  2.19 us (2%)
  between operations  1.42 us (1%)
    ppermute x3, waiting for transfers between devices, from_behind(): return lax.ppermute(block, axis, route)  31.4 us
    ppermute x3, starting transfers between devices, from_behind(): return lax.ppermute(block, axis, route)  19.8 us
    dot_general x2, matrix products, update(): jnp.einsum('kgtn,nkd->kgtd', weights.astype(jnp.bfloat16), value_rows, pr...  10.8 us
    unnamed x11, local copies, waits for them, and re-layouts  7.89 us
    reduce_sum x2, other arithmetic, update(): summed = summed * shrink + jnp.sum(weights, axis=-1)  3.25 us
    while x1, local copies, waits for them, and re-layouts, per_device(): running, _ = lax.fori_loop(1, reach + 1, advance, (running, paired))  3.23 us
    mul x1, other arithmetic, relative_gap(): return jnp.transpose(jnp.mean(difference * difference, axis=-1) / scale_sum)  2.47 us
    while x3, local copies, waits for them, and re-layouts  2.38 us
  transfers between devices with their start and end apart: 4, of which 4 were waited for; matrix products, arithmetic and copies ran while one was open for 2% of the time, Pallas kernels for 0%

commit v1 on v0

--- a/solution.py
+++ b/solution.py
@@ -1,8 +1,11 @@
+import functools
 import math
 
 import jax
 import jax.numpy as jnp
 from jax import lax
+from jax.experimental import pallas as pl
+from jax.experimental.pallas import tpu as pltpu
 from jax.sharding import PartitionSpec as P
 
 HEADS = 40
@@ -118,6 +121,256 @@
     return (outputs, gap)
 
 
+MESH = pl.DeviceIdType.MESH
+DROP = -1e30
+
+
+def kernel(sizes, lens, q_in, k_in, v_in, o_out, gap_out, q_buf, kv_own, kv_prev, kv_far, kv_pick,
+           o_buf, other, bias, gap_num, gap_den, q_sem, kv_sem, o_sem, prev_send, prev_recv, far_send,
+           far_recv, mp_send, mp_recv):
+    rows, tokens, kv_local, group = sizes
+    wide = group * HEAD_DIM
+    half = kv_local // 2
+    factor = math.log2(math.e) / math.sqrt(HEAD_DIM)
+    row = lax.axis_index("row")
+    mp = lax.axis_index("mp")
+    after = lax.rem(row + 1, rows)
+    before = lax.rem(row + rows - 1, rows)
+
+    def head_of(i):
+        return lax.rem(i + half * (1 - mp), kv_local)
+
+    def cols(i):
+        return pl.ds(pl.multiple_of(head_of(i) * HEAD_DIM, HEAD_DIM), HEAD_DIM)
+
+    def wide_cols(i):
+        return pl.ds(pl.multiple_of(head_of(i) * wide, HEAD_DIM), wide)
+
+    def local_kv(i, n):
+        src = (k_in, v_in)[n]
+        return pltpu.make_async_copy(src.at[0, :, cols(i)], kv_own.at[i, n], kv_sem.at[i, n])
+
+    def local_q(i):
+        return pltpu.make_async_copy(
+            q_in.at[0, :, wide_cols(i)], q_buf.at[:, wide_cols(i)], q_sem.at[i]
+        )
+
+    def local_o(i):
+        return pltpu.make_async_copy(
+            o_buf.at[:, wide_cols(i)], o_out.at[0, :, wide_cols(i)], o_sem.at[i]
+        )
+
+    def to_prev(i, n):
+        src = (k_in, v_in)[n]
+        return pltpu.make_async_remote_copy(
+            src_ref=src.at[0, :, cols(i)], dst_ref=kv_prev.at[i, n],
+            send_sem=prev_send.at[i, n], recv_sem=prev_recv.at[i, n],
+            device_id={"row": after}, device_id_type=MESH,
+        )
+
+    def to_far(i, n, src):
+        return pltpu.make_async_remote_copy(
+            src_ref=src, dst_ref=kv_far.at[i, n],
+            send_sem=far_send.at[i, n], recv_sem=far_recv.at[i, n],
+            device_id={"row": before}, device_id_type=MESH,
+        )
+
+    def far_own(i, n):
+        return to_far(i, n, (k_in, v_in)[n].at[0, :, cols(i)])
+
+    def to_mate(i):
+        return pltpu.make_async_remote_copy(
+            src_ref=o_buf.at[:, wide_cols(i)], dst_ref=other.at[i],
+            send_sem=mp_send.at[i], recv_sem=mp_recv.at[i],
+            device_id={"mp": 1 - mp}, device_id_type=MESH,
+        )
+
+    for i in range(kv_local):
+        for n in range(2):
+            local_kv(i, n).start()
+        local_q(i).start()
+    barrier = pltpu.get_barrier_semaphore()
+    for neighbour in (after, before):
+        pl.semaphore_signal(barrier, inc=1, device_id={"row": neighbour}, device_id_type=MESH)
+    pl.semaphore_signal(barrier, inc=1, device_id={"mp": 1 - mp}, device_id_type=MESH)
+    pl.semaphore_wait(barrier, 3)
+
+    for i in range(kv_local):
+        for n in range(2):
+            @pl.when(row == 1)
+            def _():
+                far_own(i, n).start()
+
+            @pl.when(row < rows - 1)
+            def _():
+                to_prev(i, n).start()
+
+    first, second = lens[0], lens[1]
+
+    def begin_of(block):
+        at = block * tokens
+        return jnp.where(first <= at, first, 0) + jnp.where(first + second <= at, second, 0)
+
+    qi = lax.broadcasted_iota(jnp.int32, (tokens, tokens), 0) + row * tokens
+    ki = lax.broadcasted_iota(jnp.int32, (tokens, tokens), 1) + row * tokens
+    begin = jnp.where(first <= qi, first, 0) + jnp.where(first + second <= qi, second, 0)
+    bias[0] = jnp.where((ki >= begin) & (ki <= qi), 0.0, DROP)
+    bias[1] = jnp.where(ki - tokens >= begin, 0.0, DROP)
+    bias[2] = jnp.where(ki - 2 * tokens >= begin, 0.0, DROP)
+
+    @pl.when(row == 1)
+    def _():
+        kv_far[...] = jnp.zeros_like(kv_far)
+
+    @pl.when(row == 0)
+    def _():
+        last_needs = jnp.where(begin_of(rows - 1) < (rows - 2) * tokens, 1.0, 0.0)
+        for i in range(kv_local):
+            for n in range(2):
+                local_kv(i, n).wait()
+                to_far(i, n, kv_pick.at[i, n]).wait_recv()
+                flag = jnp.broadcast_to(last_needs, (tokens, HEAD_DIM))
+                kv_pick[i, n] = jnp.where(
+                    flag > 0.5,
+                    kv_far[i, n].astype(jnp.float32),
+                    kv_own[i, n].astype(jnp.float32),
+                ).astype(jnp.bfloat16)
+                to_far(i, n, kv_pick.at[i, n]).start()
+
+    def dot_t(a, b):
+        return lax.dot_general(a, b, (((1,), (1,)), ((), ())), preferred_element_type=jnp.float32)
+
+    def dot(a, b):
+        return jnp.dot(a.astype(jnp.bfloat16), b, preferred_element_type=jnp.float32)
+
+    def head_cols(i, g):
+        at = head_of(i) * wide + g * HEAD_DIM
+        return pl.ds(pl.multiple_of(at, HEAD_DIM), HEAD_DIM)
+
+    def one_head(i, g, full):
+        at = head_cols(i, g)
+        q = q_buf[:, at]
+        near = dot_t(q, kv_own[i, 0]) + bias[0]
+        top = jnp.max(near, axis=-1, keepdims=True)
+        if full:
+            prev = dot_t(q, kv_prev[i, 0]) + bias[1]
+            far = dot_t(q, kv_far[i, 0]) + bias[2]
+            top = jnp.maximum(top, jnp.max(prev, axis=-1, keepdims=True))
+            top = jnp.maximum(top, jnp.max(far, axis=-1, keepdims=True))
+        near = jnp.exp2((near - top) * factor)
+        total = jnp.sum(near, axis=-1, keepdims=True)
+        mixed = dot(near, kv_own[i, 1])
+        if full:
+            prev = jnp.exp2((prev - top) * factor)
+            total += jnp.sum(prev, axis=-1, keepdims=True)
+            mixed += dot(prev, kv_prev[i, 1])
+            far = jnp.exp2((far - top) * factor)
+            total += jnp.sum(far, axis=-1, keepdims=True)
+            mixed += dot(far, kv_far[i, 1])
+        o_buf[:, at] = (mixed / total).astype(jnp.bfloat16)
+
+    lane = lax.broadcasted_iota(jnp.int32, (tokens, HEAD_DIM), 1)
+    gap_num[...] = jnp.zeros_like(gap_num)
+    gap_den[...] = jnp.zeros_like(gap_den)
+
+    for i in range(kv_local):
+        local_q(i).wait()
+
+        @pl.when(row == 0)
+        def _():
+            lax.fori_loop(0, group, lambda g, c: (one_head(i, g, False), c)[1], 0)
+
+        @pl.when(row > 0)
+        def _():
+            for n in range(2):
+                local_kv(i, n).wait()
+                to_prev(i, n).wait_recv()
+
+            @pl.when(row > 1)
+            def _():
+                for n in range(2):
+                    to_far(i, n, kv_far.at[i, n]).wait_recv()
+
+                    @pl.when(row == rows - 1)
+                    def _():
+                        to_far(i, n, kv_far.at[i, n]).start()
+
+            for g in range(group):
+                one_head(i, g, True)
+
+        local_o(i).start()
+        if i < half:
+            to_mate(i).start()
+        else:
+            to_mate(i - half).wait_recv()
+            for g in range(group):
+                mine = o_buf[:, head_cols(i, g)].astype(jnp.float32)
+                theirs = other[i - half, :, g * HEAD_DIM:(g + 1) * HEAD_DIM].astype(jnp.float32)
+                policy = jnp.where(mp == 0, mine, theirs)
+                apart = mine - theirs
+                here = lane == (i - half) * group + g
+                gap_num[...] = jnp.where(
+                    here, jnp.sum(apart * apart, axis=-1, keepdims=True), gap_num[...]
+                )
+                gap_den[...] = jnp.where(
+                    here, jnp.sum(policy * policy, axis=-1, keepdims=True), gap_den[...]
+                )
+    num = jnp.transpose(gap_num[...])[: half * group] / HEAD_DIM
+    den = jnp.transpose(gap_den[...])[: half * group] / HEAD_DIM
+    gap_out[...] = num / (den + 1e-06)
+
+    for i in range(kv_local):
+        local_o(i).wait()
+        if i < half:
+            to_mate(i).wait_send()
+        for n in range(2):
+            @pl.when(row < rows - 1)
+            def _():
+                to_prev(i, n).wait_send()
+
+            @pl.when(row == 1)
+            def _():
+                far_own(i, n).wait_send()
+
+            @pl.when((row == 0) | (row == rows - 1))
+            def _():
+                to_far(i, n, kv_pick.at[i, n]).wait_send()
+
+
+def fused(rows, queries, keys, values, lengths):
+    tokens = queries.shape[1]
+    kv_local = keys.shape[2] // HEAD_DIM
+    group = HEADS // KV_HEADS
+    width = queries.shape[2]
+    half = kv_local // 2
+    kv = pltpu.VMEM((kv_local, 2, tokens, HEAD_DIM), jnp.bfloat16)
+    dma = pltpu.SemaphoreType.DMA
+    return pl.pallas_call(
+        functools.partial(kernel, (rows, tokens, kv_local, group)),
+        out_shape=(
+            jax.ShapeDtypeStruct((1, tokens, width), jnp.bfloat16),
+            jax.ShapeDtypeStruct((half * group, tokens), jnp.float32),
+        ),
+        in_specs=[pl.BlockSpec(memory_space=pltpu.SMEM)] + [pl.BlockSpec(memory_space=pl.ANY)] * 3,
+        out_specs=(pl.BlockSpec(memory_space=pl.ANY), pl.BlockSpec(memory_space=pltpu.VMEM)),
+        scratch_shapes=[
+            pltpu.VMEM((tokens, width), jnp.bfloat16),
+            kv, kv, kv, kv,
+            pltpu.VMEM((tokens, width), jnp.bfloat16),
+            pltpu.VMEM((half, tokens, group * HEAD_DIM), jnp.bfloat16),
+            pltpu.VMEM((3, tokens, tokens), jnp.float32),
+            pltpu.VMEM((tokens, HEAD_DIM), jnp.float32),
+            pltpu.VMEM((tokens, HEAD_DIM), jnp.float32),
+            dma((kv_local,)), dma((kv_local, 2)), dma((kv_local,)),
+            dma((kv_local, 2)), dma((kv_local, 2)), dma((kv_local, 2)), dma((kv_local, 2)),
+            dma((half,)), dma((half,)),
+        ],
+        compiler_params=pltpu.CompilerParams(
+            collective_id=0, has_side_effects=True, vmem_limit_bytes=48 << 20
+        ),
+    )(lengths, queries, keys, values)
+
+
 def solution(mesh):
     in_specs = (
         P("mp", ("groups", "row"), "col"),
@@ -126,6 +379,13 @@
         P("groups"),
     )
     out_specs = (P("mp", ("groups", "row"), "col"), P(("col", "mp"), ("groups", "row")))
+    rows = mesh.shape["row"]
+
+    def body(queries, keys, values, lengths):
+        if lengths.shape[0] == 2 and rows == 4:
+            return fused(rows, queries, keys, values, lengths)
+        return per_device(queries, keys, values, lengths)
+
     return jax.shard_map(
-        per_device, mesh=mesh, in_specs=in_specs, out_specs=out_specs, check_vma=False
-    )
+        body, mesh=mesh, in_specs=in_specs, out_specs=out_specs, check_vma=False
+    )

time: 104 us -> 43 us (0.41); the launches traced: 102 us -> 42.8 us
  Pallas kernels: 0 us -> 36.6 us
  waiting for transfers between devices: 32.8 us -> 0 us
  starting transfers between devices: 19.8 us -> 0 us
  other arithmetic: 16.5 us -> 0 us
  matrix products: 12.7 us -> 0 us
  local copies, waits for them, and re-layouts: 16.5 us -> 5.53 us
  loops' own time: 2.19 us -> 0 us
    pallas_call x0 -> x1, Pallas kernels: none -> 36.6 us  [fused(): pl.pallas_call(functools.partial(kernel, (rows, tokens, kv_local, group))...]
    ppermute x4 -> x0, waiting for transfers between devices: 32.8 us -> none  [the longest x3 31.4 us: from_behind(): return lax.ppermute(block, axis, route)]
    ppermute x4 -> x0, starting transfers between devices: 19.8 us -> none  [the longest x3 19.8 us: from_behind(): return lax.ppermute(block, axis, route)]
    dot_general x4 -> x0, matrix products: 12.7 us -> none  [the longest x2 10.8 us: update(): jnp.einsum('kgtn,nkd->kgtd', weights.astype(jnp.bfloat16), value_rows, pr...]
    while x4 -> x0, local copies, waits for them, and re-layouts: 5.6 us -> none  [the longest x1 3.23 us: per_device(): running, _ = lax.fori_loop(1, reach + 1, advance, (running, paired))]
    reduce_sum x5 -> x0, other arithmetic: 5.5 us -> none  [the longest x2 3.25 us: update(): summed = summed * shrink + jnp.sum(weights, axis=-1)]
    mul x1 -> x0, other arithmetic: 2.47 us -> none  [relative_gap(): return jnp.transpose(jnp.mean(difference * difference, axis=-1) / scale_sum)]
    unnamed x11 -> x10, local copies, waits for them, and re-layouts: 7.89 us -> 5.53 us
  transfers between devices with their start and end apart: 4 -> 0, of which waited for: 4 -> 0; matrix products, arithmetic and copies ran while one was open for 2% -> 0% of each run, Pallas kernels for 0% -> 0%
where the time goes in v1:
time: 43 us; the launch traced here: 42.8 us
  Pallas kernels  36.6 us (85%)
  local copies, waits for them, and re-layouts  5.53 us (13%)
  between operations  0.65 us (2%)
    pallas_call x1, Pallas kernels, fused(): pl.pallas_call(functools.partial(kernel, (rows, tokens, kv_local, group))...  36.6 us
    unnamed x10, local copies, waits for them, and re-layouts  5.53 us

profile of v1, /device:TPU:18, one launch (start us, length us, event | category | flops | bytes accessed | tf_op | source)
XLA Modules:
  0.0 42.8 jit_solution(17464116894214900274)
XLA Ops:
  0.6 0.0 copy-start
  0.6 1.3 %copy-done = bf16[1,256,2560]{2,1,0:T(8,128)(2,1)S(1)} copy-done((bf16[1,256,2560]{2,1,0:T(8,128)(2,1)S(1)}, bf16[1,256,2560]{2,1,0:T(8,128)(2,1)}, u32[]{:S(2)}) %copy-start) | copy-done | bytes 1310744
  1.9 0.0 copy-start.1
  1.9 0.9 %copy-done.1 = bf16[1,256,512]{2,1,0:T(8,128)(2,1)S(1)} copy-done((bf16[1,256,512]{2,1,0:T(8,128)(2,1)S(1)}, bf16[1,256,512]{2,1,0:T(8,128)(2,1)}, u32[]{:S(2)}) %copy-start.1) | copy-done | bytes 262168
  2.9 0.0 copy-start.2
  2.9 0.9 %copy-done.2 = bf16[1,256,512]{2,1,0:T(8,128)(2,1)S(1)} copy-done((bf16[1,256,512]{2,1,0:T(8,128)(2,1)S(1)}, bf16[1,256,512]{2,1,0:T(8,128)(2,1)}, u32[]{:S(2)}) %copy-start.2) | copy-done | bytes 262168
  3.8 0.0 copy-start.3
  3.9 0.7 %copy-done.3 = s32[2]{0:T(128)S(1)} copy-done((s32[2]{0:T(128)S(1)}, s32[2]{0:T(128)}, u32[]{:S(2)}) %copy-start.3) | copy-done | bytes 32
  4.5 36.6 %shard_map.59 = (bf16[1,256,2560]{2,1,0:T(8,128)(2,1)S(1)}, f32[10,256]{1,0:T(8,128)S(1)}) custom-call(s32[2]{0:T(128)S(1)} %copy-done.3, bf16[1,256,2560]{2,1,0:T(8,128)(2,1)S(1)} %copy-done, bf16[1,256,512]{2,1,0:T(8,128)(2,1)S(1)} %copy-done.1, bf16[1,256,512]{2,1,0:T(8,128)(2,1)S(1)} %copy-done.2), custom_call_target="tpu_custom_call" | custom-call | tf_op jit(solution)/shard_map/pallas_call | solution.py:348
  41.1 1.1 %copy.8 = bf16[1,256,2560]{2,1,0:T(8,128)(2,1)} copy(bf16[1,256,2560]{2,1,0:T(8,128)(2,1)S(1)} %get-tuple-element.4) | data formatting | bytes 2621440
  42.2 0.6 %copy.9 = f32[10,256]{1,0:T(8,128)} copy(f32[10,256]{1,0:T(8,128)S(1)} %get-tuple-element.5) | data formatting | bytes 20480
Async XLA Ops:
  0.6 1.3 %copy-start = (bf16[1,256,2560]{2,1,0:T(8,128)(2,1)S(1)}, bf16[1,256,2560]{2,1,0:T(8,128)(2,1)}, u32[]{:S(2)}) copy-start(bf16[1,256,2560]{2,1,0:T(8,128)(2,1)} %q_in.1) | copy-start | bytes 3932164
  1.9 0.9 %copy-start.1 = (bf16[1,256,512]{2,1,0:T(8,128)(2,1)S(1)}, bf16[1,256,512]{2,1,0:T(8,128)(2,1)}, u32[]{:S(2)}) copy-start(bf16[1,256,512]{2,1,0:T(8,128)(2,1)} %k_in.1) | copy-start | bytes 786436
  2.9 0.9 %copy-start.2 = (bf16[1,256,512]{2,1,0:T(8,128)(2,1)S(1)}, bf16[1,256,512]{2,1,0:T(8,128)(2,1)}, u32[]{:S(2)}) copy-start(bf16[1,256,512]{2,1,0:T(8,128)(2,1)} %v_in.1) | copy-start | bytes 786436
  3.8 0.7 %copy-start.3 = (s32[2]{0:T(128)S(1)}, s32[2]{0:T(128)}, u32[]{:S(2)}) copy-start(s32[2]{0:T(128)} %lens.1) | copy-start | bytes 28

commit v2 on v1

--- a/solution.py
+++ b/solution.py
@@ -125,9 +125,9 @@
 DROP = -1e30
 
 
-def kernel(sizes, lens, q_in, k_in, v_in, o_out, gap_out, q_buf, kv_own, kv_prev, kv_far, kv_pick,
-           o_buf, other, bias, gap_num, gap_den, q_sem, kv_sem, o_sem, prev_send, prev_recv, far_send,
-           far_recv, mp_send, mp_recv):
+def kernel(sizes, lens_in, q_in, k_in, v_in, o_out, gap_out, lens, q_buf, kv_own, kv_prev, kv_far,
+           o_buf, other, bias, gap_num, gap_den, tops, totals, mixes, far_mass, lens_sem, q_sem,
+           kv_sem, o_sem, prev_send, prev_recv, far_send, far_recv, mp_send, mp_recv):
     rows, tokens, kv_local, group = sizes
     wide = group * HEAD_DIM
     half = kv_local // 2
@@ -168,15 +168,12 @@
             device_id={"row": after}, device_id_type=MESH,
         )
 
-    def to_far(i, n, src):
+    def to_far(i, n):
         return pltpu.make_async_remote_copy(
-            src_ref=src, dst_ref=kv_far.at[i, n],
+            src_ref=kv_prev.at[i, n], dst_ref=kv_far.at[i, n],
             send_sem=far_send.at[i, n], recv_sem=far_recv.at[i, n],
-            device_id={"row": before}, device_id_type=MESH,
-        )
-
-    def far_own(i, n):
-        return to_far(i, n, (k_in, v_in)[n].at[0, :, cols(i)])
+            device_id={"row": after}, device_id_type=MESH,
+        )
 
     def to_mate(i):
         return pltpu.make_async_remote_copy(
@@ -185,6 +182,8 @@
             device_id={"mp": 1 - mp}, device_id_type=MESH,
         )
 
+    lens_copy = pltpu.make_async_copy(lens_in, lens, lens_sem)
+    lens_copy.start()
     for i in range(kv_local):
         for n in range(2):
             local_kv(i, n).start()
@@ -195,47 +194,44 @@
     pl.semaphore_signal(barrier, inc=1, device_id={"mp": 1 - mp}, device_id_type=MESH)
     pl.semaphore_wait(barrier, 3)
 
-    for i in range(kv_local):
-        for n in range(2):
-            @pl.when(row == 1)
-            def _():
-                far_own(i, n).start()
-
-            @pl.when(row < rows - 1)
-            def _():
+    @pl.when(row < rows - 1)
+    def _():
+        for i in range(kv_local):
+            for n in range(2):
                 to_prev(i, n).start()
 
+    @pl.when(row == 0)
+    def _():
+        kv_prev[...] = jnp.zeros_like(kv_prev)
+
+    @pl.when(row < 2)
+    def _():
+        kv_far[...] = jnp.zeros_like(kv_far)
+
+    lens_copy.wait()
     first, second = lens[0], lens[1]
-
-    def begin_of(block):
-        at = block * tokens
-        return jnp.where(first <= at, first, 0) + jnp.where(first + second <= at, second, 0)
-
     qi = lax.broadcasted_iota(jnp.int32, (tokens, tokens), 0) + row * tokens
     ki = lax.broadcasted_iota(jnp.int32, (tokens, tokens), 1) + row * tokens
     begin = jnp.where(first <= qi, first, 0) + jnp.where(first + second <= qi, second, 0)
     bias[0] = jnp.where((ki >= begin) & (ki <= qi), 0.0, DROP)
     bias[1] = jnp.where(ki - tokens >= begin, 0.0, DROP)
     bias[2] = jnp.where(ki - 2 * tokens >= begin, 0.0, DROP)
-
-    @pl.when(row == 1)
+    gap_num[...] = jnp.zeros_like(gap_num)
+    gap_den[...] = jnp.zeros_like(gap_den)
+    for i in range(kv_local):
+        local_q(i).wait()
+        for n in range(2):
+            local_kv(i, n).wait()
+
+    @pl.when(row > 0)
     def _():
-        kv_far[...] = jnp.zeros_like(kv_far)
-
-    @pl.when(row == 0)
-    def _():
-        last_needs = jnp.where(begin_of(rows - 1) < (rows - 2) * tokens, 1.0, 0.0)
         for i in range(kv_local):
             for n in range(2):
-                local_kv(i, n).wait()
-                to_far(i, n, kv_pick.at[i, n]).wait_recv()
-                flag = jnp.broadcast_to(last_needs, (tokens, HEAD_DIM))
-                kv_pick[i, n] = jnp.where(
-                    flag > 0.5,
-                    kv_far[i, n].astype(jnp.float32),
-                    kv_own[i, n].astype(jnp.float32),
-                ).astype(jnp.bfloat16)
-                to_far(i, n, kv_pick.at[i, n]).start()
+                to_prev(i, n).wait_recv()
+
+                @pl.when(row < rows - 1)
+                def _():
+                    to_far(i, n).start()
 
     def dot_t(a, b):
         return lax.dot_general(a, b, (((1,), (1,)), ((), ())), preferred_element_type=jnp.float32)
@@ -247,74 +243,99 @@
         at = head_of(i) * wide + g * HEAD_DIM
         return pl.ds(pl.multiple_of(at, HEAD_DIM), HEAD_DIM)
 
-    def one_head(i, g, full):
+    def near_part(i, g):
+        q = q_buf[:, head_cols(i, g)]
+        own = dot_t(q, kv_own[i, 0]) + bias[0]
+        prev = dot_t(q, kv_prev[i, 0]) + bias[1]
+        top = jnp.maximum(
+            jnp.max(own, axis=-1, keepdims=True), jnp.max(prev, axis=-1, keepdims=True)
+        )
+        own = jnp.exp2((own - top) * factor)
+        prev = jnp.exp2((prev - top) * factor)
+        total = jnp.sum(own, axis=-1, keepdims=True) + jnp.sum(prev, axis=-1, keepdims=True)
+        tops[g] = jnp.broadcast_to(top, (tokens, HEAD_DIM))
+        totals[g] = jnp.broadcast_to(total, (tokens, HEAD_DIM))
+        mixes[g] = dot(own, kv_own[i, 1]) + dot(prev, kv_prev[i, 1])
+
+    def far_part(i, g):
+        q = q_buf[:, head_cols(i, g)]
+        far = dot_t(q, kv_far[i, 0]) + bias[2]
+        old = tops[g][:, :1]
+        top = jnp.maximum(old, jnp.max(far, axis=-1, keepdims=True))
+        far = jnp.exp2((far - top) * factor)
+        shrink = jnp.exp2((old - top) * factor)
+        total = totals[g][:, :1] * shrink + jnp.sum(far, axis=-1, keepdims=True)
+        totals[g] = jnp.broadcast_to(1.0 / total, (tokens, HEAD_DIM))
+        mixes[g] = mixes[g] * shrink
+        far_mass[g] = far.astype(jnp.bfloat16)
+
+    def last_part(i, g):
+        mixed = mixes[g] + dot(far_mass[g], kv_far[i, 1])
+        o_buf[:, head_cols(i, g)] = (mixed * totals[g]).astype(jnp.bfloat16)
+
+    def one_head(i, g):
         at = head_cols(i, g)
         q = q_buf[:, at]
         near = dot_t(q, kv_own[i, 0]) + bias[0]
-        top = jnp.max(near, axis=-1, keepdims=True)
-        if full:
-            prev = dot_t(q, kv_prev[i, 0]) + bias[1]
-            far = dot_t(q, kv_far[i, 0]) + bias[2]
-            top = jnp.maximum(top, jnp.max(prev, axis=-1, keepdims=True))
-            top = jnp.maximum(top, jnp.max(far, axis=-1, keepdims=True))
+        prev = dot_t(q, kv_prev[i, 0]) + bias[1]
+        far = dot_t(q, kv_far[i, 0]) + bias[2]
+        top = jnp.maximum(
+            jnp.max(near, axis=-1, keepdims=True), jnp.max(prev, axis=-1, keepdims=True)
+        )
+        top = jnp.maximum(top, jnp.max(far, axis=-1, keepdims=True))
         near = jnp.exp2((near - top) * factor)
-        total = jnp.sum(near, axis=-1, keepdims=True)
-        mixed = dot(near, kv_own[i, 1])
-        if full:
-            prev = jnp.exp2((prev - top) * factor)
-            total += jnp.sum(prev, axis=-1, keepdims=True)
-            mixed += dot(prev, kv_prev[i, 1])
-            far = jnp.exp2((far - top) * factor)
-            total += jnp.sum(far, axis=-1, keepdims=True)
-            mixed += dot(far, kv_far[i, 1])
+        prev = jnp.exp2((prev - top) * factor)
+        far = jnp.exp2((far - top) * factor)
+        total = jnp.sum(near, axis=-1, keepdims=True) + jnp.sum(prev, axis=-1, keepdims=True)
+        total += jnp.sum(far, axis=-1, keepdims=True)
+        mixed = dot(near, kv_own[i, 1]) + dot(prev, kv_prev[i, 1]) + dot(far, kv_far[i, 1])
         o_buf[:, at] = (mixed / total).astype(jnp.bfloat16)
 
+    def far_here(i, n):
+        @pl.when(row > 1)
+        def _():
+            to_far(i, n).wait_recv()
+
     lane = lax.broadcasted_iota(jnp.int32, (tokens, HEAD_DIM), 1)
-    gap_num[...] = jnp.zeros_like(gap_num)
-    gap_den[...] = jnp.zeros_like(gap_den)
-
-    for i in range(kv_local):
-        local_q(i).wait()
-
-        @pl.when(row == 0)
-        def _():
-            lax.fori_loop(0, group, lambda g, c: (one_head(i, g, False), c)[1], 0)
-
-        @pl.when(row > 0)
-        def _():
-            for n in range(2):
-                local_kv(i, n).wait()
-                to_prev(i, n).wait_recv()
-
-            @pl.when(row > 1)
-            def _():
-                for n in range(2):
-                    to_far(i, n, kv_far.at[i, n]).wait_recv()
-
-                    @pl.when(row == rows - 1)
-                    def _():
-                        to_far(i, n, kv_far.at[i, n]).start()
-
+
+    def add_gap(i):
+        for g in range(group):
+            mine = o_buf[:, head_cols(i, g)].astype(jnp.float32)
+            theirs = other[i - half, :, g * HEAD_DIM:(g + 1) * HEAD_DIM].astype(jnp.float32)
+            policy = jnp.where(mp == 0, mine, theirs)
+            apart = mine - theirs
+            here = lane == (i - half) * group + g
+            gap_num[...] = jnp.where(
+                here, jnp.sum(apart * apart, axis=-1, keepdims=True), gap_num[...]
+            )
+            gap_den[...] = jnp.where(
+                here, jnp.sum(policy * policy, axis=-1, keepdims=True), gap_den[...]
+            )
+
+    last = kv_local - 1
+    for i in range(last):
+        if i == last - 1:
             for g in range(group):
-                one_head(i, g, True)
-
+                near_part(last, g)
+        for n in range(2):
+            far_here(i, n)
+        for g in range(group):
+            one_head(i, g)
         local_o(i).start()
         if i < half:
             to_mate(i).start()
         else:
             to_mate(i - half).wait_recv()
-            for g in range(group):
-                mine = o_buf[:, head_cols(i, g)].astype(jnp.float32)
-                theirs = other[i - half, :, g * HEAD_DIM:(g + 1) * HEAD_DIM].astype(jnp.float32)
-                policy = jnp.where(mp == 0, mine, theirs)
-                apart = mine - theirs
-                here = lane == (i - half) * group + g
-                gap_num[...] = jnp.where(
-                    here, jnp.sum(apart * apart, axis=-1, keepdims=True), gap_num[...]
-                )
-                gap_den[...] = jnp.where(
-                    here, jnp.sum(policy * policy, axis=-1, keepdims=True), gap_den[...]
-                )
+            add_gap(i)
+    to_mate(last - half).wait_recv()
+    far_here(last, 0)
+    for g in range(group):
+        far_part(last, g)
+    far_here(last, 1)
+    for g in range(group):
+        last_part(last, g)
+    local_o(last).start()
+    add_gap(last)
     num = jnp.transpose(gap_num[...])[: half * group] / HEAD_DIM
     den = jnp.transpose(gap_den[...])[: half * group] / HEAD_DIM
     gap_out[...] = num / (den + 1e-06)
@@ -328,13 +349,9 @@
             def _():
                 to_prev(i, n).wait_send()
 
-            @pl.when(row == 1)
+            @pl.when((row > 0) & (row < rows - 1))
             def _():
-                far_own(i, n).wait_send()
-
-            @pl.when((row == 0) | (row == rows - 1))
-            def _():
-                to_far(i, n, kv_pick.at[i, n]).wait_send()
+                to_far(i, n).wait_send()
 
 
 def fused(rows, queries, keys, values, lengths):
@@ -351,17 +368,22 @@
             jax.ShapeDtypeStruct((1, tokens, width), jnp.bfloat16),
             jax.ShapeDtypeStruct((half * group, tokens), jnp.float32),
         ),
-        in_specs=[pl.BlockSpec(memory_space=pltpu.SMEM)] + [pl.BlockSpec(memory_space=pl.ANY)] * 3,
+        in_specs=[pl.BlockSpec(memory_space=pltpu.HBM)] * 4,
         out_specs=(pl.BlockSpec(memory_space=pl.ANY), pl.BlockSpec(memory_space=pltpu.VMEM)),
         scratch_shapes=[
+            pltpu.SMEM((2,), jnp.int32),
             pltpu.VMEM((tokens, width), jnp.bfloat16),
-            kv, kv, kv, kv,
+            kv, kv, kv,
             pltpu.VMEM((tokens, width), jnp.bfloat16),
             pltpu.VMEM((half, tokens, group * HEAD_DIM), jnp.bfloat16),
             pltpu.VMEM((3, tokens, tokens), jnp.float32),
             pltpu.VMEM((tokens, HEAD_DIM), jnp.float32),
             pltpu.VMEM((tokens, HEAD_DIM), jnp.float32),
-            dma((kv_local,)), dma((kv_local, 2)), dma((kv_local,)),
+            pltpu.VMEM((group, tokens, HEAD_DIM), jnp.float32),
+            pltpu.VMEM((group, tokens, HEAD_DIM), jnp.float32),
+            pltpu.VMEM((group, tokens, HEAD_DIM), jnp.float32),
+            pltpu.VMEM((group, tokens, tokens), jnp.bfloat16),
+            dma, dma((kv_local,)), dma((kv_local, 2)), dma((kv_local,)),
             dma((kv_local, 2)), dma((kv_local, 2)), dma((kv_local, 2)), dma((kv_local, 2)),
             dma((half,)), dma((half,)),
         ],

time: 43 us -> 36.6 us (0.85)
  Pallas kernels: 36.6 us -> 30.2 us
    pallas_call x1, Pallas kernels: 36.6 us -> 30.2 us  [fused(): pl.pallas_call(functools.partial(kernel, (rows, tokens, kv_local, group))...]
where the time goes in v2:
time: 36.6 us; the launch traced here: 36.4 us
  Pallas kernels  30.2 us (83%)
  local copies, waits for them, and re-layouts  5.53 us (15%)
  between operations  0.65 us (2%)
    pallas_call x1, Pallas kernels, fused(): pl.pallas_call(functools.partial(kernel, (rows, tokens, kv_local, group))...  30.2 us
    unnamed x10, local copies, waits for them, and re-layouts  5.53 us

profile of v2, /device:TPU:18, one launch (start us, length us, event | category | flops | bytes accessed | tf_op | source)
XLA Modules:
  0.0 36.4 jit_solution(2058039258615985965)
XLA Ops:
  0.6 0.0 copy-start
  0.6 1.3 %copy-done = bf16[1,256,2560]{2,1,0:T(8,128)(2,1)S(1)} copy-done((bf16[1,256,2560]{2,1,0:T(8,128)(2,1)S(1)}, bf16[1,256,2560]{2,1,0:T(8,128)(2,1)}, u32[]{:S(2)}) %copy-start) | copy-done | bytes 1310744
  1.9 0.0 copy-start.1
  1.9 0.9 %copy-done.1 = bf16[1,256,512]{2,1,0:T(8,128)(2,1)S(1)} copy-done((bf16[1,256,512]{2,1,0:T(8,128)(2,1)S(1)}, bf16[1,256,512]{2,1,0:T(8,128)(2,1)}, u32[]{:S(2)}) %copy-start.1) | copy-done | bytes 262168
  2.9 0.0 copy-start.2
  2.9 0.9 %copy-done.2 = bf16[1,256,512]{2,1,0:T(8,128)(2,1)S(1)} copy-done((bf16[1,256,512]{2,1,0:T(8,128)(2,1)S(1)}, bf16[1,256,512]{2,1,0:T(8,128)(2,1)}, u32[]{:S(2)}) %copy-start.2) | copy-done | bytes 262168
  3.8 0.0 copy-start.3
  3.9 0.7 %copy-done.3 = s32[2]{0:T(128)S(1)} copy-done((s32[2]{0:T(128)S(1)}, s32[2]{0:T(128)}, u32[]{:S(2)}) %copy-start.3) | copy-done | bytes 32
  4.5 30.2 %shard_map.59 = (bf16[1,256,2560]{2,1,0:T(8,128)(2,1)S(1)}, f32[10,256]{1,0:T(8,128)S(1)}) custom-call(s32[2]{0:T(128)S(1)} %copy-done.3, bf16[1,256,2560]{2,1,0:T(8,128)(2,1)S(1)} %copy-done, bf16[1,256,512]{2,1,0:T(8,128)(2,1)S(1)} %copy-done.1, bf16[1,256,512]{2,1,0:T(8,128)(2,1)S(1)} %copy-done.2), custom_call_target="tpu_custom_call" | custom-call | tf_op jit(solution)/shard_map/pallas_call | solution.py:365
  34.8 1.1 %copy.8 = bf16[1,256,2560]{2,1,0:T(8,128)(2,1)} copy(bf16[1,256,2560]{2,1,0:T(8,128)(2,1)S(1)} %get-tuple-element.4) | data formatting | bytes 2621440
  35.8 0.6 %copy.9 = f32[10,256]{1,0:T(8,128)} copy(f32[10,256]{1,0:T(8,128)S(1)} %get-tuple-element.5) | data formatting | bytes 20480
Async XLA Ops:
  0.6 1.3 %copy-start = (bf16[1,256,2560]{2,1,0:T(8,128)(2,1)S(1)}, bf16[1,256,2560]{2,1,0:T(8,128)(2,1)}, u32[]{:S(2)}) copy-start(bf16[1,256,2560]{2,1,0:T(8,128)(2,1)} %q_in.1) | copy-start | bytes 3932164
  1.9 0.9 %copy-start.1 = (bf16[1,256,512]{2,1,0:T(8,128)(2,1)S(1)}, bf16[1,256,512]{2,1,0:T(8,128)(2,1)}, u32[]{:S(2)}) copy-start(bf16[1,256,512]{2,1,0:T(8,128)(2,1)} %k_in.1) | copy-start | bytes 786436
  2.9 0.9 %copy-start.2 = (bf16[1,256,512]{2,1,0:T(8,128)(2,1)S(1)}, bf16[1,256,512]{2,1,0:T(8,128)(2,1)}, u32[]{:S(2)}) copy-start(bf16[1,256,512]{2,1,0:T(8,128)(2,1)} %v_in.1) | copy-start | bytes 786436
  3.8 0.7 %copy-start.3 = (s32[2]{0:T(128)S(1)}, s32[2]{0:T(128)}, u32[]{:S(2)}) copy-start(s32[2]{0:T(128)} %lens_in.1) | copy-start | bytes 28

commit v3 on v2

--- a/solution.py
+++ b/solution.py
@@ -388,7 +388,7 @@
             dma((half,)), dma((half,)),
         ],
         compiler_params=pltpu.CompilerParams(
-            collective_id=0, has_side_effects=True, vmem_limit_bytes=48 << 20
+            collective_id=0, has_side_effects=True, vmem_limit_bytes=67043328
         ),
     )(lengths, queries, keys, values)
 

time: 36.6 us -> 35 us (0.956)
  local copies, waits for them, and re-layouts: 5.53 us -> 3.07 us
  Pallas kernels: 30.2 us -> 31.1 us
    unnamed x10 -> x4, local copies, waits for them, and re-layouts: 5.53 us -> 3.07 us
    pallas_call x1, Pallas kernels: 30.2 us -> 31.1 us  [fused(): pl.pallas_call(functools.partial(kernel, (rows, tokens, kv_local, group))...]
where the time goes in v3:
time: 35 us; the launch traced here: 34.8 us
  Pallas kernels  31.1 us (89%)
  local copies, waits for them, and re-layouts  3.07 us (9%)
  between operations  0.65 us (2%)
    pallas_call x1, Pallas kernels, fused(): pl.pallas_call(functools.partial(kernel, (rows, tokens, kv_local, group))...  31.1 us
    unnamed x4, local copies, waits for them, and re-layouts  3.07 us

profile of v3, /device:TPU:18, one launch (start us, length us, event | category | flops | bytes accessed | tf_op | source)
XLA Modules:
  0.0 34.8 jit_solution(11841992867335795008)
XLA Ops:
  0.6 31.1 %shard_map.59 = (bf16[1,256,2560]{2,1,0:T(8,128)(2,1)}, f32[10,256]{1,0:T(8,128)}) custom-call(s32[2]{0:T(128)} %lens_in.1, bf16[1,256,2560]{2,1,0:T(8,128)(2,1)} %q_in.1, bf16[1,256,512]{2,1,0:T(8,128)(2,1)} %k_in.1, bf16[1,256,512]{2,1,0:T(8,128)(2,1)} %v_in.1), custom_call_target="tpu_custom_call" | custom-call | tf_op jit(solution)/shard_map/pallas_call | solution.py:365
  31.7 0.0 copy-start
  31.7 2.5 %copy.8 = bf16[1,256,2560]{2,1,0:T(8,128)(2,1)} copy(bf16[1,256,2560]{2,1,0:T(8,128)(2,1)} %get-tuple-element.4) | data formatting | bytes 2621440
  34.2 0.0 copy-done
  34.2 0.6 %copy.9 = f32[10,256]{1,0:T(8,128)} copy(f32[10,256]{1,0:T(8,128)S(1)} %copy-done) | data formatting | bytes 20480
Async XLA Ops:
  31.7 2.5 %copy-start = (f32[10,256]{1,0:T(8,128)S(1)}, f32[10,256]{1,0:T(8,128)}, u32[]{:S(2)}) copy-start(f32[10,256]{1,0:T(8,128)} %get-tuple-element.5) | copy-start | bytes 30724
